TPU v7x, 256 devices: a whole 4x4x8 slice. The times are simulated.
256 devices in a mesh: group: 16 (over y, x), member: 16 (over z, core).
Axes of the slice: x: 4, y: 4, z: 8, core: 2. Of those that a mesh axis runs over, the one named last changes fastest.
Arguments:
- test_points: bfloat16 [256, 3, 1024], P(('group', 'member')), may hold values from 0 to 4
- test_basis: bfloat16 [256, 2, 1024, 256], P(('group', 'member')), may hold values from -0.25 to 0.25
- source_points: bfloat16 [256, 3, 1024], P(('group', 'member')), may hold values from 0 to 4
- source_basis: bfloat16 [256, 2, 1024, 256], P(('group', 'member')), may hold values from -0.1875 to 0.1875
- excitation: bfloat16 [256, 2, 256, 256], P(('group', 'member')), may hold values from -6 to 6
- preconditioner: bfloat16 [256, 256, 2, 256], P(('group', 'member')), may hold values from -0.25 to 0.25
- plan: int32 [2, 2], replicated, may hold values from 0 to 255, as said below
- solver_owner: int32 [256, 2, 4], P(('group', 'member')), may hold values from 0 to 15, as said below
Outputs:
- result: float32 [256, 256, 2, 256], P(('group', 'member'))
Inputs may be any that keep to these rules, and one draw needn't show every extreme that they name: `plan`: distinct domain indices. `solver_owner`: owners lie in the tile's own group. At most 2 of one device's 8 tiles go to one owner; in every group one owner takes exactly 2 tiles from every device of the group.
All inputs are finite; a program needn't handle non-finite values.
Results may differ from a plain program's by a relative error of at most 0.008.
Values may be sent and summed in bfloat16 or wider, within the bound.
A program may use at most 128 MiB of HBM per device.

v0:
```python
import math

import jax
import jax.numpy as jnp
from jax import lax
from jax.sharding import PartitionSpec as P

CAP = 2


wave_number = 2.0 * math.pi
wire_radius = 0.05


def spread(value, axis, source):
    kept = jnp.where(lax.axis_index(axis) == source, value, 0).astype(value.dtype)
    return lax.psum(kept, axis)


def green_joined(points_test, points_source):
    near = points_test.astype(jnp.float32)
    far = points_source.astype(jnp.float32)
    dist_sq = jnp.zeros((near.shape[1], far.shape[1]), jnp.float32)
    for component in range(3):
        offset = near[component][:, None] - far[component][None, :]
        dist_sq = dist_sq + offset * offset
    distance = jnp.sqrt(dist_sq + wire_radius * wire_radius)
    weight = 1.0 / (4.0 * math.pi * distance)
    green_re = (jnp.cos(wave_number * distance) * weight).astype(jnp.bfloat16)
    green_im = (-jnp.sin(wave_number * distance) * weight).astype(jnp.bfloat16)
    return jnp.concatenate([green_re, green_im], axis=1)


def complex_block(real_part, imag_part):
    upper = jnp.concatenate([real_part, imag_part], axis=1)
    lower = jnp.concatenate([-imag_part, real_part], axis=1)
    return jnp.concatenate([upper, lower], axis=0)


def shards(
    test_points,
    test_basis,
    source_points,
    source_basis,
    excitation,
    preconditioner,
    plan,
    solver_owner,
):
    members = lax.axis_size("member")
    n_basis = source_basis.shape[3]
    n_excite = excitation.shape[3]
    own_points = test_points[0]
    own_basis = test_basis[0]
    domains_here = solver_owner.shape[1]
    per_domain = own_basis.shape[1] // domains_here
    owners = plan.reshape(-1)
    n_sources = owners.shape[0]
    bundle = (source_points[0], source_basis[0], excitation[0])
    left_basis = jnp.concatenate(
        [
            own_basis[0].reshape(domains_here, per_domain, n_basis),
            own_basis[1].reshape(domains_here, per_domain, n_basis),
        ],
        axis=1,
    )
    reduced_list = []
    coeff_list = []
    for source_slot in range(n_sources):
        owner_index = owners[source_slot]
        arrived = (
            spread(bundle[0], ("group", "member"), owner_index),
            spread(bundle[1], ("group", "member"), owner_index),
            spread(bundle[2], ("group", "member"), owner_index),
        )
        far_points, far_basis, far_coeff = arrived
        green = green_joined(own_points, far_points)
        basis_block = complex_block(far_basis[0], far_basis[1])
        half_field = jnp.dot(green, basis_block, preferred_element_type=jnp.float32).astype(
            jnp.bfloat16
        )
        half_split = half_field.reshape(domains_here, per_domain, 2 * n_basis)
        half_re = half_split[:, :, :n_basis]
        half_im = half_split[:, :, n_basis:]
        right_side = jnp.concatenate(
            [half_split, jnp.concatenate([half_im, -half_re], axis=2)], axis=1
        )
        reduced = jnp.einsum(
            "dpb,dpc->dbc", left_basis, right_side, preferred_element_type=jnp.float32
        ).astype(jnp.bfloat16)
        reduced_list.append(reduced)
        coeff_list.append(far_coeff)
    owner_ids = solver_owner[0].T.reshape(-1)
    tile_total = owner_ids.shape[0]
    all_tiles = jnp.concatenate(reduced_list, axis=0).reshape(tile_total, 2 * n_basis * n_basis)
    source_ids = jnp.arange(tile_total, dtype=jnp.int32) // domains_here
    same_owner = (owner_ids[:, None] == owner_ids[None, :]).astype(jnp.int32)
    lower_mask = (jnp.arange(tile_total)[None, :] < jnp.arange(tile_total)[:, None]).astype(
        jnp.int32
    )
    earlier = jnp.sum(same_owner * lower_mask, axis=1)
    slot_index = owner_ids * CAP + earlier
    placing = (slot_index[None, :] == jnp.arange(members * CAP, dtype=jnp.int32)[:, None]).astype(
        jnp.int32
    )
    packed = jnp.dot(
        placing.astype(jnp.bfloat16), all_tiles, preferred_element_type=jnp.float32
    ).astype(jnp.bfloat16)
    packed = packed.reshape(members, CAP, 2 * n_basis * n_basis)
    used = jnp.sum(placing, axis=1)
    labels = jnp.sum(placing * source_ids[None, :], axis=1) + (1 - used) * n_sources
    labels = labels.astype(jnp.float32).astype(jnp.bfloat16).reshape(members, CAP)
    got_tiles, got_labels = (
        lax.all_to_all(packed, "member", split_axis=0, concat_axis=0, tiled=True),
        lax.all_to_all(labels, "member", split_axis=0, concat_axis=0, tiled=True),
    )
    flat_tiles = got_tiles.reshape(members * CAP, 2 * n_basis * n_basis)
    flat_labels = got_labels.reshape(-1)
    wanted = jnp.arange(n_sources, dtype=jnp.float32).astype(jnp.bfloat16)
    picking = (flat_labels[None, :] == wanted[:, None]).astype(jnp.bfloat16)
    summed = jnp.dot(picking, flat_tiles, preferred_element_type=jnp.float32)
    summed = summed.reshape(n_sources, n_basis, 2 * n_basis)
    summed_high = summed.astype(jnp.bfloat16)
    summed_rest = (summed - summed_high.astype(jnp.float32)).astype(jnp.bfloat16)
    excite_all = jnp.stack([complex_block(coeff[0], coeff[1]) for coeff in coeff_list], axis=0)
    assembled = jnp.einsum(
        "sbk,ske->be", summed_high, excite_all, preferred_element_type=jnp.float32
    )
    assembled = assembled + jnp.einsum(
        "sbk,ske->be", summed_rest, excite_all, preferred_element_type=jnp.float32
    )
    assembled_low = assembled.astype(jnp.bfloat16)
    z_block = complex_block(assembled_low[:, :n_excite], assembled_low[:, n_excite:])
    inverse_rows = preconditioner[0].reshape(n_basis, 2 * n_basis)
    outcome = jnp.dot(inverse_rows, z_block, preferred_element_type=jnp.float32)
    return outcome.reshape(1, n_basis, 2, n_excite)


def solution(mesh):
    return jax.shard_map(
        shards,
        mesh=mesh,
        in_specs=(
            P(("group", "member"), None, None),
            P(("group", "member"), None, None, None),
            P(("group", "member"), None, None),
            P(("group", "member"), None, None, None),
            P(("group", "member"), None, None, None),
            P(("group", "member"), None, None, None),
            P(),
            P(("group", "member"), None, None),
        ),
        out_specs=P(("group", "member"), None, None, None),
        check_vma=False,
    )
```

profile of v0, /device:TPU:1, one launch (start us, length us, event | category | flops | bytes accessed | tf_op | source)
XLA Modules:
  0.0 550.1 jit_solution(15854012212366830386)
XLA Ops:
  6.5 0.8 copy.28
  8.4 10.0 %all-to-all-start = ((bf16[16,1,2]{2,1,0:T(2,128)(2,1)}), bf16[16,1,2]{2,1,0:T(2,128)(2,1)S(1)}, u32[]{:S(2)}, u32[]{:S(2)}) async-start(bf16[16,1,2]{2,1,0:T(2,128)(2,1)} %convert_element_type.170), calls=%async_computation | async-start | bytes 16384 | tf_op jit(solution)/shard_map/all_to_all | solution.py:115
  18.4 0.8 reshape.153
  22.3 3.3 select_bitcast_fusion.3
  25.6 1.0 select_bitcast_fusion.7
  27.8 78.1 %all-reduce = (bf16[3,1024]{1,0:T(4,128)(2,1)S(1)}, bf16[3,1024]{1,0:T(4,128)(2,1)S(1)}, bf16[3,1024]{1,0:T(4,128)(2,1)S(1)}, bf16[3,1024]{1,0:T(4,128)(2,1)S(1)}) all-reduce(bf16[3,1024]{1,0:T(4,128)(2,1)S(1)} %get-tuple-element.88, ...), channel_id=1, replica_groups=mesh['group'=16,'member'=16] {'group','member'}, use_global_device_ids=true, to_apply=%region_3.4 | all-reduce | flops 12288 | bytes 49152 | tf_op jit(solution)/shard_map/psum | solution.py:17
  105.9 80.0 %multiply_convert_fusion.7 = (bf16[1024,1024]{1,0:T(8,128)(2,1)}, bf16[1024,1024]{1,0:T(8,128)(2,1)}, bf16[1024,1024]{1,0:T(8,128)(2,1)}, bf16[1024,1024]{1,0:T(...) fusion(f32[1024]{0:T(1024)S(1)} %bitcast.156, ...), kind=kLoop, calls=%fused_computation.33 | loop fusion | flops 71303168 | bytes 16838656 | tf_op jit(solution)/shard_map/convert_element_type | solution.py:29
  185.9 116.6 %all-reduce.4.cloned.1.call-done = (bf16[2,1024,256]{2,1,0:T(8,128)(2,1)}, bf16[2,1024,256]{2,1,0:T(8,128)(2,1)}, bf16[2,1024,256]{2,1,0:T(8,128)(2,1)}, bf16[2,...) async-done(((bf16[2,1024,256]{2,1,0:T(8,128)(2,1)}, ...) | async-done | bytes 5242896 | tf_op jit(solution)/shard_map/psum | solution.py:17
  302.5 1.8 slice_bitcast_fusion
  305.5 0.9 copy-done.19
  307.0 2.3 fusion.71
  309.5 2.3 fusion.76
  311.9 2.3 fusion.81
  314.4 2.3 fusion.86
  319.9 1.2 copy.37
  321.1 5.0 convolution_convert_fusion
  326.1 9.4 %reshape.159 = bf16[16,2,131072]{2,1,0:T(2,128)(2,1)} reshape(bf16[32,131072]{1,0:T(8,128)(2,1)} %convolution_convert_fusion) | data formatting | bytes 16777216 | tf_op jit(solution)/shard_map/reshape | solution.py:109
  335.5 8.2 %all-to-all-start.1 = ((bf16[16,2,131072]{2,1,0:T(2,128)(2,1)}), bf16[16,2,131072]{2,1,0:T(2,128)(2,1)}, u32[]{:S(2)}, u32[]{:S(2)}) async-start(bf16[16,2,131072]{2,1,0:T(2,128)(2,1)} %reshape.159), calls=%async_computation.1 | async-start | bytes 16777216 | tf_op jit(solution)/shard_map/all_to_all | solution.py:114
  344.2 182.8 %all-to-all-done.1 = bf16[16,2,131072]{2,1,0:T(2,128)(2,1)} async-done(((bf16[16,2,131072]{2,1,0:T(2,128)(2,1)}), bf16[16,2,131072]{2,1,0:T(2,128)(2,1)}, u32[]{:S(2)}, u32[]{:S(2)}) %all-to-all-start.1) | async-done | bytes 8388640 | tf_op jit(solution)/shard_map/all_to_all | solution.py:114
  527.1 8.5 %reshape.160 = bf16[32,131072]{1,0:T(8,128)(2,1)} reshape(bf16[16,2,131072]{2,1,0:T(2,128)(2,1)} %all-to-all-done.1) | data formatting | bytes 16777216 | tf_op jit(solution)/shard_map/reshape | solution.py:117
  535.6 4.7 subtract_convert_fusion
  540.3 0.8 convolution_bitcast_fusion
  541.1 0.8 fusion.104
  542.2 1.0 copy.35
  (84 shorter events, 8.9 us)
Async XLA Ops:
  6.5 19.1 %copy-start.9 = (bf16[1,2,256,256]{3,2,1,0:T(8,128)(2,1)S(1)}, bf16[1,2,256,256]{3,2,1,0:T(8,128)(2,1)}, u32[]{:S(2)}) copy-start(bf16[1,2,256,256]{3,2,1,0:T(8,128)(2,1)} %param.12) | copy-start | bytes 786436
  8.4 327.1 %all-to-all-start = ((bf16[16,1,2]{2,1,0:T(2,128)(2,1)}), bf16[16,1,2]{2,1,0:T(2,128)(2,1)S(1)}, u32[]{:S(2)}, u32[]{:S(2)}) async-start(bf16[16,1,2]{2,1,0:T(2,128)(2,1)} %convert_element_type.170), calls=%async_computation | async-start | bytes 16384 | tf_op jit(solution)/shard_map/all_to_all | solution.py:115
  18.4 284.1 %all-reduce.4.cloned.1.call-start = ((), (), s32[]{:S(2)}) async-start(), calls=%async_computation.2 | async-start | bytes 10485760 | tf_op jit(solution)/shard_map/psum | solution.py:17
  25.6 1.0 copy-start.12
  25.6 1.1 copy-start.11
  25.6 1.6 copy-start.4
  302.5 1.9 copy-start.2
  302.5 2.2 copy-start.3
  302.5 2.5 copy-start
  302.5 2.8 copy-start.1
  304.7 1.7 copy-start.19
  304.7 2.4 copy-start.20
  307.0 2.4 copy-start.17
  307.0 2.4 copy-start.18
  309.5 2.4 copy-start.15
  309.5 2.4 copy-start.16
  311.9 2.4 copy-start.13
  311.9 2.4 copy-start.14
  335.5 8.2 %copy-start.10 = (bf16[1,256,2,256]{3,2,1,0:T(2,128)(2,1)S(1)}, bf16[1,256,2,256]{3,2,1,0:T(2,128)(2,1)}, u32[]{:S(2)}) copy-start(bf16[1,256,2,256]{3,2,1,0:T(2,128)(2,1)} %param.13) | copy-start | bytes 786436
  335.5 8.4 %copy-start.7 = (bf16[2,256,256]{2,1,0:T(8,128)(2,1)S(1)}, bf16[2,256,256]{2,1,0:T(8,128)(2,1)}, u32[]{:S(2)}) copy-start(bf16[2,256,256]{2,1,0:T(8,128)(2,1)} %get-tuple-element.15) | copy-start | bytes 786436
  335.5 8.4 %copy-start.8 = (bf16[2,256,256]{2,1,0:T(8,128)(2,1)S(1)}, bf16[2,256,256]{2,1,0:T(8,128)(2,1)}, u32[]{:S(2)}) copy-start(bf16[2,256,256]{2,1,0:T(8,128)(2,1)} %get-tuple-element.16) | copy-start | bytes 786436
  335.5 8.6 %copy-start.5 = (bf16[2,256,256]{2,1,0:T(8,128)(2,1)S(1)}, bf16[2,256,256]{2,1,0:T(8,128)(2,1)}, u32[]{:S(2)}) copy-start(bf16[2,256,256]{2,1,0:T(8,128)(2,1)} %get-tuple-element.17) | copy-start | bytes 786436
  335.5 8.6 %copy-start.6 = (bf16[2,256,256]{2,1,0:T(8,128)(2,1)S(1)}, bf16[2,256,256]{2,1,0:T(8,128)(2,1)}, u32[]{:S(2)}) copy-start(bf16[2,256,256]{2,1,0:T(8,128)(2,1)} %get-tuple-element.18) | copy-start | bytes 786436
  335.5 191.6 %all-to-all-start.1 = ((bf16[16,2,131072]{2,1,0:T(2,128)(2,1)}), bf16[16,2,131072]{2,1,0:T(2,128)(2,1)}, u32[]{:S(2)}, u32[]{:S(2)}) async-start(bf16[16,2,131072]{2,1,0:T(2,128)(2,1)} %reshape.159), calls=%async_computation.1 | async-start | bytes 16777216 | tf_op jit(solution)/shard_map/all_to_all | solution.py:114
Sparse Core Ops, SparseCore 0:
  26.8 275.6 all-reduce.3
where the time goes:
time: 551 us; the launch traced here: 550 us
  waiting for transfers between devices  299 us (54%)
  other arithmetic  85.5 us (16%)
  blocking collectives  78.1 us (14%)
  local copies, waits for them, and re-layouts  28.8 us (5%)
  matrix products  23.7 us (4%)
  starting transfers between devices  18.2 us (3%)
  between operations  16.3 us (3%)
    all_to_all x1, waiting for transfers between devices, shards(): lax.all_to_all(packed, 'member', split_axis=0, concat_axis=0, tiled=True)  183 us
    psum x1, waiting for transfers between devices, spread(): return lax.psum(kept, axis)  117 us
    convert_element_type x1, other arithmetic, green_joined(): green_re = (jnp.cos(wave_number * distance) * weight).astype(jnp.bfloat16)  80 us
    psum x1, blocking collectives, spread(): return lax.psum(kept, axis)  78.1 us
  transfers between devices with their start and end apart: 3, of which 2 were waited for; matrix products, arithmetic and copies ran while one was open for 21% of the time, Pallas kernels for 0%

commit v1 on v0

v1 whole, which is shorter than its diff:
```python
import functools
import math

import jax
import jax.numpy as jnp
from jax import lax
from jax.experimental import pallas as pl
from jax.experimental.pallas import tpu as pltpu
from jax.sharding import PartitionSpec as P

MESH = pl.DeviceIdType.MESH
BF = jnp.bfloat16
F32 = jnp.float32

SIN = (0.07765591, -0.59829041, 2.55007739, -5.16771008, 3.14159264)
COS = (0.21968242, -1.33187297, 4.05841079, -4.9347928, 0.99999995)
RADIUS_SQ = 0.05 * 0.05

PTS = 1024
NB = 256
NX, NY, NZ = 4, 4, 8
PLANE = NX * NY * 2


def poly(coefficients, u):
    total = coefficients[0] * u + coefficients[1]
    for value in coefficients[2:]:
        total = total * u + value
    return total


def split3(value):
    high = value.astype(BF).astype(F32)
    rest = value - high
    mid = rest.astype(BF).astype(F32)
    return high, mid, rest - mid


def augment(points, store, is_source):
    centred = points.astype(F32) - 2.0
    h, m, l = split3(centred)
    size = jnp.sum(centred * centred, axis=0, keepdims=True)
    if not is_source:
        size = size + RADIUS_SQ
    sh, sm, sl = split3(size)
    ones = jnp.ones_like(sh)
    if is_source:
        parts = (h, m, h, m, l, h)
        tail = (ones, ones, ones, sh, sm, sl)
    else:
        parts = tuple(-2.0 * v for v in (h, h, m, m, h, l))
        tail = (sh, sm, sl, ones, ones, ones)
    row = 0
    for part in parts:
        store[row:row + 3, :] = part
        row += 3
    for part in tail:
        store[row:row + 1, :] = part
        row += 1
    store[row:row + 8, :] = jnp.zeros((8, part.shape[1]), F32)


def body(
    plan, owner_smem, owner_vec, test_pts, kb, src_pts, jb, xb,
    zblk,
    bundle, recv1, sel, recv2, fin, full,
    pt_recv, pt_sel, pt_z, test_all, kall, owner_rem, owner_other,
    aug_stage, aug_test, aug_src, d2buf, gre, gim, prod,
    pair_snd, pair_rcv, ch_snd, ch_rcv, table,
    p1_s, p1_r, s1_s, s1_r, p2_s, p2_r, s2_s, s2_r, s3_s, s3_r,
    s4_s, s4_r, k_s, k_r, pair_s, pair_r, ch_s, ch_r, loc,
):
    g = lax.axis_index("group")
    m = lax.axis_index("member")
    x, y = lax.rem(g, NX), lax.div(g, NX)
    c, z = lax.rem(m, 2), lax.div(m, 2)
    q = g * 2 + c
    other = 1 - c
    partner = (g, z * 2 + other)

    def remote(src, dst, send, recv, device):
        return pltpu.make_async_remote_copy(
            src_ref=src, dst_ref=dst, send_sem=send, recv_sem=recv,
            device_id=device, device_id_type=MESH,
        )

    def plane_peer(i):
        target = lax.rem(q + i, PLANE)
        return lax.div(target, 2), lax.rem(target, 2)

    def member_peer(i):
        return lax.rem(m + i, 2 * NZ)

    barrier = pltpu.get_barrier_semaphore()

    @pl.loop(1, PLANE)
    def _(i):
        tg, tc = plane_peer(i)
        pl.semaphore_signal(barrier, inc=1, device_id=(tg, z * 2 + tc), device_id_type=MESH)

    @pl.loop(1, 2 * NZ)
    def _(i):
        pl.semaphore_signal(barrier, inc=1, device_id=(g, member_peer(i)), device_id_type=MESH)

    pl.semaphore_wait(barrier, PLANE - 1 + 2 * NZ - 1)

    @pl.loop(1, PLANE)
    def _(i):
        tg, tc = plane_peer(i)
        remote(src_pts, pt_recv.at[q], p1_s, p1_r, (tg, z * 2 + tc)).start()

    pt_recv[q] = src_pts[...]

    k_copies = [
        remote(test_pts, test_all.at[1], k_s.at[0], k_r.at[0], partner),
        remote(owner_vec, owner_rem, k_s.at[1], k_r.at[1], partner),
    ]
    for copy in k_copies:
        copy.start()
    test_all[0] = test_pts[...]

    @pl.loop(0, 4)
    def _(b):
        rows = pl.ds(pl.multiple_of(b * 256, 256), 256)
        jr, ji = jb[0, rows, :], jb[1, rows, :]
        xr, xi = xb[0], xb[1]
        dot = functools.partial(jnp.dot, preferred_element_type=F32)
        re = dot(jr, xr) - dot(ji, xi)
        im = dot(jr, xi) + dot(ji, xr)
        bundle[pl.ds(b * 4, 4), :, 0:NB] = re.astype(BF).reshape(4, 64, NB)
        bundle[pl.ds(b * 4, 4), :, NB:2 * NB] = im.astype(BF).reshape(4, 64, NB)

    def half_cols(which):
        return pl.ds(pl.multiple_of(which * NB, NB), NB)

    @pl.loop(1, PLANE)
    def _(i):
        tg, tc = plane_peer(i)
        remote(
            bundle.at[tg, :, half_cols(tc)], recv1.at[q], s1_s, s1_r, (tg, z * 2 + tc)
        ).start()

    keep = pltpu.make_async_copy(bundle.at[g, :, half_cols(c)], recv1.at[q], loc.at[0])
    keep.start()

    k_big = remote(kb, kall.at[1], k_s.at[2], k_r.at[2], partner)
    k_big.start()
    k_own = pltpu.make_async_copy(kb, kall.at[0], loc.at[1])
    k_own.start()

    def wait_bytes(ref, send, recv):
        done = remote(ref, ref, send, recv, partner)
        done.wait_recv()
        done.wait_send()

    wait_bytes(pt_recv.at[pl.ds(0, PLANE - 1)], p1_s, p1_r)

    def plane_of(owner):
        return lax.div(owner, 2 * NZ) * 2 + lax.rem(owner, 2)

    def z_of(owner):
        return lax.div(lax.rem(owner, 2 * NZ), 2)

    for s in range(2):
        pt_sel[s] = pt_recv[plane_of(plan[c, s])]

    @pl.loop(1, NZ)
    def _(i):
        tz = lax.rem(z + i, NZ)
        remote(pt_sel, pt_z.at[z], p2_s, p2_r, (g, tz * 2 + c)).start()

    for s in range(2):
        pt_z[z, s] = pt_sel[s]

    wait_bytes(recv1.at[pl.ds(0, PLANE - 1)], s1_s, s1_r)
    keep.wait()
    for j in range(4):
        qj = plane_of(plan[j // 2, j % 2])
        for zp in range(NZ):
            r0, c0 = (zp % 4) * 16, (zp // 4) * 128
            sel[zp * 4 + j] = recv1[qj, r0:r0 + 16, c0:c0 + 128]

    @pl.loop(1, NZ)
    def _(i):
        tz = lax.rem(z + i, NZ)
        remote(
            sel.at[pl.ds(tz * 4, 4)], recv2.at[pl.ds(z * 4, 4)], s2_s, s2_r, (g, tz * 2 + c)
        ).start()

    recv2[pl.ds(z * 4, 4)] = sel[pl.ds(z * 4, 4)]

    wait_bytes(pt_z.at[pl.ds(0, NZ - 1)], p2_s, p2_r)
    k_copies[0].wait_recv()
    for s in range(2):
        augment(pt_z[z_of(plan[c, s]), s], aug_stage, True)
        aug_src[s] = aug_stage[...].astype(BF)
        augment(test_all[s], aug_stage, False)
        aug_test[s] = aug_stage[...].astype(BF)

    def green(first, last):
        @pl.loop(first, last)
        def _(unit):
            s, rest = lax.div(unit, 8), lax.rem(unit, 8)
            who, blk = lax.div(rest, 4), lax.rem(rest, 4)
            rows = pl.ds(pl.multiple_of(blk * 256, 256), 256)
            d2buf[...] = lax.dot_general(
                aug_test[who, :, rows], aug_src[s],
                (((0,), (0,)), ((), ())), preferred_element_type=F32,
            )
            base = rest * 256

            @pl.loop(0, 16)
            def _(r):
                row = pl.ds(pl.multiple_of(r * 16, 16), 16)
                out = pl.ds(pl.multiple_of(base + r * 16, 16), 16)
                for col in range(0, PTS, 512):
                    d2 = jnp.maximum(d2buf[row, col:col + 512], RADIUS_SQ)
                    inv = lax.rsqrt(d2)
                    dist = d2 * inv
                    f = dist - jnp.round(dist)
                    u = f * f
                    sn = poly(SIN, u) * f
                    cs = poly(COS, u)
                    t = (inv * (0.5 / math.pi)) * sn
                    re = inv * (0.25 / math.pi) - t * sn
                    gre[s, out, col:col + 512] = re.astype(BF)
                    gim[s, out, col:col + 512] = (t * cs).astype(BF)

    green(0, 3)

    wait_bytes(recv2.at[pl.ds(0, 4 * (NZ - 1))], s2_s, s2_r)
    for j in range(4):
        fin[j] = recv2[z_of(plan[j // 2, j % 2]) * 4 + j]

    my_rows = pl.ds(pl.multiple_of(lax.rem(z, 4) * 16, 16), 16)
    my_cols = pl.ds(pl.multiple_of(c * NB + lax.div(z, 4) * 128, 128), 128)
    home = full.at[:, y, x, my_rows, my_cols]

    @pl.loop(1, 2 * NZ)
    def _(i):
        tm = member_peer(i)
        remote(fin.at[pl.ds(lax.rem(tm, 2) * 2, 2)], home, s3_s, s3_r, (g, tm)).start()

    keep3 = pltpu.make_async_copy(fin.at[pl.ds(c * 2, 2)], home, loc.at[2])
    keep3.start()
    green(3, 6)
    wait_bytes(recv2.at[pl.ds(0, 2 * (2 * NZ - 1))], s3_s, s3_r)
    keep3.wait()

    cols = (slice(0, NB), slice(NB, 2 * NB))

    def at_y(value):
        return (value * NX + x, m)

    def at_x(value):
        return (y * NX + value, m)

    xp, xm = lax.rem(x + 1, NX), lax.rem(x + NX - 1, NX)
    yp, ym = lax.rem(y + 1, NY), lax.rem(y + NY - 1, NY)
    started = []

    def send4(ref, index, device):
        copy = remote(ref, ref, s4_s.at[index], s4_r.at[index], device)
        copy.start()
        started.append(copy)
        return copy

    up, down = pl.ds(0, 32), pl.ds(32, 32)
    a = [
        send4(full.at[:, y, x, :, cols[0]], 0, at_y(yp)),
        send4(full.at[:, y, x, :, cols[0]], 1, at_y(ym)),
        send4(full.at[:, y, x, :, cols[1]], 2, at_x(xp)),
        send4(full.at[:, y, x, :, cols[1]], 3, at_x(xm)),
    ]
    green(6, 8)
    a[0].wait_recv()
    b = [send4(full.at[:, ym, x, up, cols[0]], 4, at_y(yp))]
    a[2].wait_recv()
    b.append(send4(full.at[:, y, xm, up, cols[1]], 5, at_x(xp)))
    a[1].wait_recv()
    b.append(send4(full.at[:, yp, x, down, cols[0]], 6, at_y(ym)))
    a[3].wait_recv()
    b.append(send4(full.at[:, y, xp, down, cols[1]], 7, at_x(xm)))
    green(8, 10)
    for copy in b:
        copy.wait_recv()
    d = []
    for s in range(2):
        k = 8 + 8 * s
        d.append([
            send4(full.at[s, :, x, :, cols[0]], k, at_x(xp)),
            send4(full.at[s, :, x, :, cols[0]], k + 1, at_x(xm)),
            send4(full.at[s, y, :, :, cols[1]], k + 2, at_y(yp)),
            send4(full.at[s, y, :, :, cols[1]], k + 3, at_y(ym)),
        ])
    lo, hi = pl.ds(0, 2), pl.ds(2, 2)
    e = []
    green(10, 13)
    for s in range(2):
        k = 12 + 8 * s
        d[s][0].wait_recv()
        e.append(send4(full.at[s, lo, xm, :, cols[0]], k, at_x(xp)))
        d[s][2].wait_recv()
        e.append(send4(full.at[s, ym, lo, :, cols[1]], k + 1, at_y(yp)))
        d[s][1].wait_recv()
        e.append(send4(full.at[s, hi, xp, :, cols[0]], k + 2, at_x(xm)))
        d[s][3].wait_recv()
        e.append(send4(full.at[s, yp, hi, :, cols[1]], k + 3, at_y(ym)))
        green(13 + 2 * s, 15 + s)
    k_big.wait_recv()
    k_own.wait()

    for s in range(2):
        for copy in e[4 * s:4 * s + 4]:
            copy.wait_recv()

        @pl.loop(0, 4)
        def _(dom, s=s):
            rows = pl.ds(pl.multiple_of(dom * 512, 512), 512)
            who = lax.div(dom, 2)
            krow = pl.ds(pl.multiple_of(lax.rem(dom, 2) * 512, 512), 512)
            basis = full[s].reshape(PTS, 2 * NB)
            dot = functools.partial(jnp.dot, preferred_element_type=F32)
            one = dot(gre[s, rows, :], basis)
            two = dot(gim[s, rows, :], basis)
            half_re = (one[:, :NB] + two[:, NB:]).astype(BF)
            half_im = (one[:, NB:] - two[:, :NB]).astype(BF)
            right = jnp.concatenate([half_re, half_im], axis=1)
            turned = jnp.concatenate([half_im, -half_re], axis=1)
            over = (((0,), (0,)), ((), ()))
            prod[s * 4 + dom] = lax.dot_general(
                kall[who, 0, krow, :], right, over, preferred_element_type=F32
            ) + lax.dot_general(
                kall[who, 1, krow, :], turned, over, preferred_element_type=F32
            )

    k_copies[1].wait_recv()
    scal = pltpu.make_async_copy(owner_rem, owner_other, loc.at[3])
    scal.start()

    @pl.loop(0, NB // 16)
    def _(i):
        prod[8, pl.ds(pl.multiple_of(i * 16, 16), 16), :] = jnp.zeros((16, 2 * NB), F32)

    scal.wait()
    owners = []
    for s in range(2):
        for dom in range(4):
            ref = owner_smem if dom < 2 else owner_other
            owners.append(ref[dom % 2, 2 * c + s])

    @pl.loop(0, 2 * NZ)
    def _(slot):
        chosen = [jnp.int32(8)] * 4
        for t in range(7, -1, -1):
            hit = owners[t] == slot
            chosen = [
                jnp.where(hit, new, old)
                for old, new in zip(chosen, [jnp.int32(t)] + chosen[:3])
            ]
        for k in range(4):
            table[slot * 4 + k] = chosen[k]

    def combine(write, zz, cc, start, count, extras):
        base = (zz * 2 + cc) * 4
        picks = [table[base + k] for k in range(4)]

        @pl.loop(0, count // 16)
        def _(i):
            near = pl.ds(pl.multiple_of(i * 16, 16), 16)
            rows = pl.ds(pl.multiple_of(start + i * 16, 16), 16)
            total = prod[picks[0], rows, :] + prod[picks[1], rows, :]
            total = total + (prod[picks[2], rows, :] + prod[picks[3], rows, :])
            for ref, shifted in extras:
                total = total + ref[near if shifted else rows, :].astype(F32)
            write(near, rows, total)

    def to_slot(dz):
        return lax.rem(z + dz + NZ, NZ)

    pair_copies = {}

    def pair_send(dz):
        zz = to_slot(dz)
        index = dz % NZ

        def write(near, rows, total):
            pair_snd[index, rows, :] = total.astype(BF)

        combine(write, zz, other, 0, NB, ())
        copy = remote(
            pair_snd.at[index], pair_rcv.at[index],
            pair_s.at[index], pair_r.at[index], partner,
        )
        copy.start()
        pair_copies[index] = copy

    waited = set()

    def pair_ready(dz):
        index = dz % NZ
        if index not in waited:
            waited.add(index)
            pair_copies[index].wait_recv()
        return pair_rcv.at[index]

    ahead = (g, lax.rem(z + 1, NZ) * 2 + c)
    behind = (g, lax.rem(z + NZ - 1, NZ) * 2 + c)
    chains = ((4, 0, ahead), (3, 128, ahead), (-4, 128, behind), (-3, 0, behind))
    ch_copies = {}

    def chain_step(ch, k):
        far, start, device = chains[ch]
        steps = abs(far)
        if k >= steps:
            return
        dz = far - k if far > 0 else far + k
        extras = [(pair_ready(dz), False)]
        if k:
            ch_copies[ch, k - 1].wait_recv()
            extras.append((ch_rcv.at[ch, k - 1], True))

        def write(near, rows, total):
            ch_snd[ch, k, near, :] = total.astype(BF)

        combine(write, to_slot(dz), c, start, 128, extras)
        copy = remote(
            ch_snd.at[ch, k], ch_rcv.at[ch, k],
            ch_s.at[4 * ch + k], ch_r.at[4 * ch + k], device,
        )
        copy.start()
        ch_copies[ch, k] = copy

    order = (0, 2, 1, 3)
    pair_send(4)
    pair_send(3)
    pair_send(-3)
    for ch in order:
        chain_step(ch, 0)
    pair_send(2)
    pair_send(-2)
    for ch in order:
        chain_step(ch, 1)
    pair_send(1)
    pair_send(-1)
    pair_send(0)
    for ch in order:
        chain_step(ch, 2)
    for ch in order:
        chain_step(ch, 3)

    own = pair_ready(0)
    for start, last, side in ((0, (0, 3), (3, 2)), (128, (2, 3), (1, 2))):
        ch_copies[side].wait_recv()
        ch_copies[last].wait_recv()

        def write(near, rows, total):
            low = total.astype(BF)
            zr, zi = low[:, :NB], low[:, NB:]
            zblk[rows, :NB] = zr
            zblk[rows, NB:] = zi
            lower = pl.ds(pl.multiple_of(rows.start + NB, 16), 16)
            zblk[lower, :NB] = -zi
            zblk[lower, NB:] = zr

        combine(
            write, z, c, start, 128,
            [(own, False), (ch_rcv.at[side[0], side[1]], True),
             (ch_rcv.at[last[0], last[1]], True)],
        )

    for copy in k_copies + [k_big] + started:
        copy.wait_send()
    for copy in list(pair_copies.values()) + list(ch_copies.values()):
        copy.wait_send()


def reduced(test_points, test_basis, source_points, source_basis, excitation, plan, owner):
    vmem = pl.BlockSpec(memory_space=pltpu.VMEM)
    smem = pl.BlockSpec(memory_space=pltpu.SMEM)
    dma = pltpu.SemaphoreType.DMA
    scratch = [
        pltpu.VMEM((16, 64, 2 * NB), BF),
        pltpu.VMEM((PLANE, 64, NB), BF),
        pltpu.VMEM((4 * NZ, 16, 128), BF),
        pltpu.VMEM((4 * NZ, 16, 128), BF),
        pltpu.VMEM((4, 16, 128), BF),
        pltpu.VMEM((2, NY, NX, 64, 2 * NB), BF),
        pltpu.VMEM((PLANE, 3, PTS), BF),
        pltpu.VMEM((2, 3, PTS), BF),
        pltpu.VMEM((NZ, 2, 3, PTS), BF),
        pltpu.VMEM((2, 3, PTS), BF),
        pltpu.VMEM((2, 2, PTS, NB), BF),
        pltpu.VMEM((2, 4), jnp.int32),
        pltpu.SMEM((2, 4), jnp.int32),
        pltpu.VMEM((32, PTS), F32),
        pltpu.VMEM((2, 32, PTS), BF),
        pltpu.VMEM((2, 32, PTS), BF),
        pltpu.VMEM((256, PTS), F32),
        pltpu.VMEM((2, 2 * PTS, PTS), BF),
        pltpu.VMEM((2, 2 * PTS, PTS), BF),
        pltpu.VMEM((9, NB, 2 * NB), F32),
        pltpu.VMEM((NZ, NB, 2 * NB), BF),
        pltpu.VMEM((NZ, NB, 2 * NB), BF),
        pltpu.VMEM((4, 4, 128, 2 * NB), BF),
        pltpu.VMEM((4, 4, 128, 2 * NB), BF),
        pltpu.SMEM((4 * 2 * NZ,), jnp.int32),
        dma, dma, dma, dma, dma, dma, dma, dma, dma, dma,
        dma((24,)), dma((24,)), dma((3,)), dma((3,)),
        dma((NZ,)), dma((NZ,)), dma((16,)), dma((16,)), dma((4,)),
    ]
    return pl.pallas_call(
        body,
        out_shape=jax.ShapeDtypeStruct((2 * NB, 2 * NB), BF),
        in_specs=[
            smem, smem, vmem, vmem, pl.BlockSpec(memory_space=pl.ANY), vmem, vmem, vmem,
        ],
        out_specs=vmem,
        scratch_shapes=scratch,
        compiler_params=pltpu.CompilerParams(
            collective_id=0, has_side_effects=True, vmem_limit_bytes=60 * 1024 * 1024
        ),
    )(plan, owner, owner, test_points, test_basis, source_points, source_basis, excitation)


def shards(
    test_points,
    test_basis,
    source_points,
    source_basis,
    excitation,
    preconditioner,
    plan,
    solver_owner,
):
    block = reduced(
        test_points[0], test_basis[0], source_points[0], source_basis[0], excitation[0],
        plan, solver_owner[0],
    )
    rows = preconditioner[0].reshape(NB, 2 * NB)
    outcome = jnp.dot(rows, block, preferred_element_type=F32)
    return outcome.reshape(1, NB, 2, NB)


def solution(mesh):
    return jax.shard_map(
        shards,
        mesh=mesh,
        in_specs=(
            P(("group", "member"), None, None),
            P(("group", "member"), None, None, None),
            P(("group", "member"), None, None),
            P(("group", "member"), None, None, None),
            P(("group", "member"), None, None, None),
            P(("group", "member"), None, None, None),
            P(),
            P(("group", "member"), None, None),
        ),
        out_specs=P(("group", "member"), None, None, None),
        check_vma=False,
    )
```

time: 551 us -> 107 us (0.19)
  waiting for transfers between devices: 299 us -> 0 us
  Pallas kernels: 0 us -> 104 us
  other arithmetic: 85.5 us -> 0 us
  blocking collectives: 78.1 us -> 0 us
  local copies, waits for them, and re-layouts: 28.8 us -> 1.98 us
  matrix products: 23.7 us -> 1.38 us
  starting transfers between devices: 18.2 us -> 0 us
  between operations: 16.3 us -> 0.02 us
    all_to_all x2 -> x0, waiting for transfers between devices: 183 us -> none  [the longest x1 183 us: shards(): lax.all_to_all(packed, 'member', split_axis=0, concat_axis=0, tiled=True)]
    psum x1 -> x0, waiting for transfers between devices: 117 us -> none  [spread(): return lax.psum(kept, axis)]
    pallas_call x0 -> x1, Pallas kernels: none -> 104 us  [reduced(): pl.pallas_call(body, out_shape=jax.ShapeDtypeStruct((2 * NB, 2 * NB), BF)...]
    convert_element_type x2 -> x0, other arithmetic: 80 us -> none  [the longest x1 80 us: green_joined(): green_re = (jnp.cos(wave_number * distance) * weight).astype(jnp.bfloat16)]
    psum x1 -> x0, blocking collectives: 78.1 us -> none  [spread(): return lax.psum(kept, axis)]
    dot_general x13 -> x1, matrix products: 23.7 us -> 1.38 us  [shards(): outcome = jnp.dot(rows, block, preferred_element_type=F32)]
    reshape x5 -> x1, local copies, waits for them, and re-layouts: 19.8 us -> 1 us  [shards(): return outcome.reshape(1, NB, 2, NB)]
    all_to_all x2 -> x0, starting transfers between devices: 18.1 us -> none  [the longest x1 9.97 us: shards(): lax.all_to_all(labels, 'member', split_axis=0, concat_axis=0, tiled=True)]
  transfers between devices with their start and end apart: 3 -> 0, of which waited for: 2 -> 0; matrix products, arithmetic and copies ran while one was open for 21% -> 0% of each run, Pallas kernels for 0% -> 0%
where the time goes in v1:
time: 107 us
  Pallas kernels  104 us (97%)
  local copies, waits for them, and re-layouts  1.98 us (2%)
  matrix products  1.38 us (1%)
    pallas_call x1, Pallas kernels, reduced(): pl.pallas_call(body, out_shape=jax.ShapeDtypeStruct((2 * NB, 2 * NB), BF)...  104 us

profile of v1, /device:TPU:1, one launch (start us, length us, event | category | flops | bytes accessed | tf_op | source)
XLA Modules:
  0.0 107.1 jit_solution(4872686778155907915)
XLA Ops:
  0.0 1.0 copy.10
  1.0 103.7 %shard_map.82 = bf16[512,512]{1,0:T(8,128)(2,1)} custom-call(s32[2,2]{1,0:T(2,128)} %plan.1, s32[2,4]{1,0:T(2,128)} %bitcast.22, s32[2,4]{1,0:T(2,128)} %bitcast.23, bf16[3,1024]{1,0:T(4,128)(2,1)} %bitcast.20, bf16[2,1024,256]{2,1,0:T(8,128)(2,1)} %bitcast.15, bf16[3,1024]{1,0:T(4,128)(2,1)} %bitcast.21, bf16[2,1024,256]{2,1,0:T(8,128)(2,1)} %bitcast.16, ...), custom_call_target="tpu_custom_call" | custom-call | tf_op jit(solution)/shard_map/pallas_call | solution.py:512
  104.7 1.4 %fusion = f32[512,256]{1,0:T(8,128)S(1)} fusion(bf16[512,512]{1,0:T(8,128)(2,1)} %shard_map.82, bf16[256,512]{1,0:T(8,128)(2,1)S(1)} %bitcast.17), kind=kOutput, calls=%fused_computation | convolution fusion | flops 134217728 | bytes 1310720 | tf_op jit(solution)/shard_map/dot_general | solution.py:541
  106.1 1.0 copy.9

commit v2 on v1

v2 whole, which is shorter than its diff:
```python
import functools
import math

import jax
import jax.numpy as jnp
from jax import lax
from jax.experimental import pallas as pl
from jax.experimental.pallas import tpu as pltpu
from jax.sharding import PartitionSpec as P

MESH = pl.DeviceIdType.MESH
BF = jnp.bfloat16
F32 = jnp.float32

SIN = (0.07765591, -0.59829041, 2.55007739, -5.16771008, 3.14159264)
COS = (0.21968242, -1.33187297, 4.05841079, -4.9347928, 0.99999995)
RADIUS_SQ = 0.05 * 0.05

PTS = 1024
NB = 256
HALF = NB // 2
NX, NY, NZ = 4, 4, 8
PLANE = NX * NY * 2


def poly(coefficients, u):
    total = coefficients[0] * u + coefficients[1]
    for value in coefficients[2:]:
        total = total * u + value
    return total


def split3(value):
    high = value.astype(BF).astype(F32)
    rest = value - high
    mid = rest.astype(BF).astype(F32)
    return high, mid, rest - mid


def augment(points, store, is_source):
    centred = points.astype(F32) - 2.0
    h, m, l = split3(centred)
    size = jnp.sum(centred * centred, axis=0, keepdims=True)
    if not is_source:
        size = size + RADIUS_SQ
    sh, sm, sl = split3(size)
    ones = jnp.ones_like(sh)
    if is_source:
        parts = (h, m, h, m, l, h)
        tail = (ones, ones, ones, sh, sm, sl)
    else:
        parts = tuple(-2.0 * v for v in (h, h, m, m, h, l))
        tail = (sh, sm, sl, ones, ones, ones)
    row = 0
    for part in parts:
        store[row:row + 3, :] = part
        row += 3
    for part in tail:
        store[row:row + 1, :] = part
        row += 1
    store[row:row + 8, :] = jnp.zeros((8, part.shape[1]), F32)


def body(
    plan, owner_smem, owner_vec, test_pts, kb, src_pts, jb_hbm, xb_hbm,
    zblk,
    jb, xb, bundle, recv1, sel, recv2, fin, full,
    pt_recv, pt_sel, pt_z, test_all, kall, owner_rem, owner_other,
    aug_stage, aug_test, aug_src, d2buf, gre, gim, prod,
    pair_snd, pair_rcv, ch_snd, ch_rcv, table,
    p1_s, p1_r, s1_s, s1_r, p2_s, p2_r, s2_s, s2_r, s3_s, s3_r,
    s4_s, s4_r, k_s, k_r, pair_s, pair_r, ch_s, ch_r, loc,
):
    g = lax.axis_index("group")
    m = lax.axis_index("member")
    x, y = lax.rem(g, NX), lax.div(g, NX)
    c, z = lax.rem(m, 2), lax.div(m, 2)
    q = g * 2 + c
    other = 1 - c
    partner = (g, z * 2 + other)
    dot = functools.partial(jnp.dot, preferred_element_type=F32)

    def remote(src, dst, send, recv, device):
        return pltpu.make_async_remote_copy(
            src_ref=src, dst_ref=dst, send_sem=send, recv_sem=recv,
            device_id=device, device_id_type=MESH,
        )

    def plane_peer(i):
        target = lax.rem(q + i, PLANE)
        return lax.div(target, 2), lax.rem(target, 2)

    def member_peer(i):
        return lax.rem(m + i, 2 * NZ)

    loads = [
        pltpu.make_async_copy(jb_hbm, jb, loc.at[0]),
        pltpu.make_async_copy(xb_hbm, xb, loc.at[1]),
    ]
    for copy in loads:
        copy.start()

    barrier = pltpu.get_barrier_semaphore()

    @pl.loop(1, 2 * NZ)
    def _(i):
        pl.semaphore_signal(barrier, inc=1, device_id=(g, member_peer(i)), device_id_type=MESH)

    @pl.loop(1, PLANE)
    def _(i):
        tg, tc = plane_peer(i)
        pl.semaphore_signal(barrier, inc=1, device_id=(tg, z * 2 + tc), device_id_type=MESH)

    for copy in loads:
        copy.wait()
    k_own = pltpu.make_async_copy(kb, kall.at[0], loc.at[2])
    k_own.start()

    @pl.loop(0, 4)
    def _(b):
        rows = pl.ds(pl.multiple_of(b * 256, 256), 256)
        jr, ji = jb[0, rows, :], jb[1, rows, :]
        xr, xi = xb[0], xb[1]
        re = (dot(jr, xr) - dot(ji, xi)).astype(BF)
        im = (dot(jr, xi) + dot(ji, xr)).astype(BF)
        for h in range(2):
            cols = slice(h * HALF, (h + 1) * HALF)
            bundle[h, pl.ds(b * 4, 4), :, 0:HALF] = re[:, cols].reshape(4, 64, HALF)
            bundle[h, pl.ds(b * 4, 4), :, HALF:NB] = im[:, cols].reshape(4, 64, HALF)

    pt_recv[q] = src_pts[...]
    test_all[0] = test_pts[...]

    pl.semaphore_wait(barrier, PLANE - 1 + 2 * NZ - 1)

    @pl.loop(1, PLANE)
    def _(i):
        tg, tc = plane_peer(i)
        remote(src_pts, pt_recv.at[q], p1_s, p1_r, (tg, z * 2 + tc)).start()

    for tc in range(2):
        @pl.when(c != tc)
        def _(tc=tc):
            remote(bundle.at[tc, g], recv1.at[q], s1_s, s1_r, (g, z * 2 + tc)).start()

        @pl.loop(1, NX * NY)
        def _(i, tc=tc):
            tg = lax.rem(g + i, NX * NY)
            remote(bundle.at[tc, tg], recv1.at[q], s1_s, s1_r, (tg, z * 2 + tc)).start()

    keep = pltpu.make_async_copy(bundle.at[c, g], recv1.at[q], loc.at[0])
    keep.start()

    k_copies = [
        remote(test_pts, test_all.at[1], k_s.at[0], k_r.at[0], partner),
        remote(owner_vec, owner_rem, k_s.at[1], k_r.at[1], partner),
        remote(kb, kall.at[1], k_s.at[2], k_r.at[2], partner),
    ]
    for copy in k_copies:
        copy.start()

    def wait_bytes(ref, send, recv):
        done = remote(ref, ref, send, recv, partner)
        done.wait_recv()
        done.wait_send()

    wait_bytes(pt_recv.at[pl.ds(0, PLANE - 1)], p1_s, p1_r)

    def plane_of(owner):
        return lax.div(owner, 2 * NZ) * 2 + lax.rem(owner, 2)

    def z_of(owner):
        return lax.div(lax.rem(owner, 2 * NZ), 2)

    for s in range(2):
        pt_sel[s] = pt_recv[plane_of(plan[c, s])]

    @pl.loop(1, NZ)
    def _(i):
        tz = lax.rem(z + i, NZ)
        remote(pt_sel, pt_z.at[z], p2_s, p2_r, (g, tz * 2 + c)).start()

    for s in range(2):
        pt_z[z, s] = pt_sel[s]

    k_copies[0].wait_recv()
    for s in range(2):
        augment(test_all[s], aug_stage, False)
        aug_test[s] = aug_stage[...].astype(BF)

    def recv_bytes(ref, recv):
        remote(ref, ref, s1_s, recv, partner).wait_recv()

    recv_bytes(recv1.at[pl.ds(0, PLANE - 1)], s1_r)
    keep.wait()
    for j in range(4):
        qj = plane_of(plan[j // 2, j % 2])
        for zp in range(NZ):
            r0, c0 = (zp % 4) * 16, (zp // 4) * 128
            sel[zp * 4 + j] = recv1[qj, r0:r0 + 16, c0:c0 + 128]

    @pl.loop(1, NZ)
    def _(i):
        tz = lax.rem(z + i, NZ)
        remote(
            sel.at[pl.ds(tz * 4, 4)], recv2.at[pl.ds(z * 4, 4)], s2_s, s2_r, (g, tz * 2 + c)
        ).start()

    recv2[pl.ds(z * 4, 4)] = sel[pl.ds(z * 4, 4)]

    wait_bytes(pt_z.at[pl.ds(0, NZ - 1)], p2_s, p2_r)
    for s in range(2):
        augment(pt_z[z_of(plan[c, s]), s], aug_stage, True)
        aug_src[s] = aug_stage[...].astype(BF)

    def green(first, last):
        @pl.loop(first, last)
        def _(unit):
            s, rest = lax.div(unit, 8), lax.rem(unit, 8)
            who, blk = lax.div(rest, 4), lax.rem(rest, 4)
            rows = pl.ds(pl.multiple_of(blk * 256, 256), 256)
            d2buf[...] = lax.dot_general(
                aug_test[who, :, rows], aug_src[s],
                (((0,), (0,)), ((), ())), preferred_element_type=F32,
            )
            base = rest * 256

            @pl.loop(0, 16)
            def _(r):
                row = pl.ds(pl.multiple_of(r * 16, 16), 16)
                out = pl.ds(pl.multiple_of(base + r * 16, 16), 16)
                for col in range(0, PTS, 512):
                    d2 = jnp.maximum(d2buf[row, col:col + 512], RADIUS_SQ)
                    inv = lax.rsqrt(d2)
                    dist = d2 * inv
                    f = dist - jnp.round(dist)
                    u = f * f
                    sn = poly(SIN, u) * f
                    cs = poly(COS, u)
                    t = (inv * (0.5 / math.pi)) * sn
                    re = inv * (0.25 / math.pi) - t * sn
                    gre[s, out, col:col + 512] = re.astype(BF)
                    gim[s, out, col:col + 512] = (t * cs).astype(BF)

    green(0, 2)

    wait_bytes(recv2.at[pl.ds(0, 4 * (NZ - 1))], s2_s, s2_r)
    for j in range(4):
        fin[j] = recv2[z_of(plan[j // 2, j % 2]) * 4 + j]

    my_rows = pl.ds(pl.multiple_of(lax.rem(z, 4) * 16, 16), 16)
    my_cols = pl.ds(pl.multiple_of(lax.div(z, 4) * 128, 128), 128)
    home = full.at[:, c, y, x, my_rows, my_cols]

    @pl.loop(1, 2 * NZ)
    def _(i):
        tm = member_peer(i)
        remote(
            fin.at[pl.ds(lax.rem(tm, 2) * 2, 2)], home, s3_s, s3_r.at[c], (g, tm)
        ).start()

    pltpu.make_async_copy(fin.at[pl.ds(c * 2, 2)], home, s3_r.at[c]).start()

    started = []
    arriving = {}

    def gather(h, stage):
        for pipe in range(2):
            along_y = pipe == stage
            if stage == 0:
                part = full.at[pipe, h, y, x]
            elif pipe == 0:
                part = full.at[0, h, :, x]
            else:
                part = full.at[1, h, y]
            for step in (1, 3, 2):
                if along_y:
                    device = (lax.rem(y + step, NY) * NX + x, m)
                else:
                    device = (y * NX + lax.rem(x + step, NX), m)
                index = ((h * 2 + stage) * 2 + pipe) * 3 + step - 1
                copy = remote(part, part, s4_s.at[index], s4_r.at[index], device)
                copy.start()
                started.append(copy)
                arriving.setdefault((h, stage), []).append(copy)

    def gathered(h, stage):
        for copy in arriving[h, stage]:
            copy.wait_recv()

    green(2, 6)
    recv_bytes(recv2.at[pl.ds(0, 2 * NZ)], s3_r.at[0])
    gather(0, 0)
    green(6, 8)
    recv_bytes(recv2.at[pl.ds(0, 2 * NZ)], s3_r.at[1])
    gather(1, 0)
    gathered(0, 0)
    gather(0, 1)
    green(8, 11)
    gathered(1, 0)
    gather(1, 1)
    green(11, 16)

    k_copies[1].wait_recv()
    scal = pltpu.make_async_copy(owner_rem, owner_other, loc.at[3])
    scal.start()
    for h in range(2):
        @pl.loop(0, NB // 16)
        def _(i, h=h):
            prod[h, 8, pl.ds(pl.multiple_of(i * 16, 16), 16), :] = jnp.zeros((16, NB), F32)

    scal.wait()
    owners = []
    for s in range(2):
        for dom in range(4):
            ref = owner_smem if dom < 2 else owner_other
            owners.append(ref[dom % 2, 2 * c + s])

    @pl.loop(0, 2 * NZ)
    def _(slot):
        chosen = [jnp.int32(8)] * 4
        for t in range(7, -1, -1):
            hit = owners[t] == slot
            chosen = [
                jnp.where(hit, new, old)
                for old, new in zip(chosen, [jnp.int32(t)] + chosen[:3])
            ]
        for k in range(4):
            table[slot * 4 + k] = chosen[k]

    k_copies[2].wait_recv()
    k_own.wait()

    def multiply(h, first, last):
        @pl.loop(first, last)
        def _(unit):
            s, dom = lax.div(unit, 4), lax.rem(unit, 4)
            rows = pl.ds(pl.multiple_of(dom * 512, 512), 512)
            who = lax.div(dom, 2)
            krow = pl.ds(pl.multiple_of(lax.rem(dom, 2) * 512, 512), 512)
            basis = full[s, h].reshape(PTS, NB)
            one = dot(gre[s, rows, :], basis)
            two = dot(gim[s, rows, :], basis)
            half_re = (one[:, :HALF] + two[:, HALF:]).astype(BF)
            half_im = (one[:, HALF:] - two[:, :HALF]).astype(BF)
            right = jnp.concatenate([half_re, half_im], axis=1)
            turned = jnp.concatenate([half_im, -half_re], axis=1)
            over = (((0,), (0,)), ((), ()))
            prod[h, unit] = lax.dot_general(
                kall[who, 0, krow, :], right, over, preferred_element_type=F32
            ) + lax.dot_general(
                kall[who, 1, krow, :], turned, over, preferred_element_type=F32
            )

    def combine(h, write, zz, cc, start, count, extras):
        base = (zz * 2 + cc) * 4
        picks = [table[base + k] for k in range(4)]

        @pl.loop(0, count // 32)
        def _(i):
            near = pl.ds(pl.multiple_of(i * 32, 32), 32)
            rows = pl.ds(pl.multiple_of(start + i * 32, 32), 32)
            total = prod[h, picks[0], rows, :] + prod[h, picks[1], rows, :]
            total = total + (prod[h, picks[2], rows, :] + prod[h, picks[3], rows, :])
            for ref, shifted in extras:
                total = total + ref[near if shifted else rows, :].astype(F32)
            write(near, rows, total)

    def to_slot(dz):
        return lax.rem(z + dz + NZ, NZ)

    pair_copies = {}
    waited = set()

    def pair_send(h, *distances):
        for dz in distances:
            index = h * NZ + dz % NZ

            def write(near, rows, total):
                pair_snd[index, rows, :] = total.astype(BF)

            combine(h, write, to_slot(dz), other, 0, NB, ())
            copy = remote(
                pair_snd.at[index], pair_rcv.at[index],
                pair_s.at[index], pair_r.at[index], partner,
            )
            copy.start()
            pair_copies[index] = copy

    def pair_ready(h, dz):
        index = h * NZ + dz % NZ
        if index not in waited:
            waited.add(index)
            pair_copies[index].wait_recv()
        return pair_rcv.at[index]

    ahead = (g, lax.rem(z + 1, NZ) * 2 + c)
    behind = (g, lax.rem(z + NZ - 1, NZ) * 2 + c)
    chains = ((4, 0, ahead), (3, 128, ahead), (-4, 128, behind), (-3, 0, behind))
    ch_copies = {}

    def chain_steps(h, k):
        for ch in (0, 2, 1, 3):
            far, start, device = chains[ch]
            if k >= abs(far):
                continue
            dz = far - k if far > 0 else far + k
            extras = [(pair_ready(h, dz), False)]
            index = (h * 4 + ch) * 4 + k
            if k:
                ch_copies[h, ch, k - 1].wait_recv()
                extras.append((ch_rcv.at[index - 1], True))

            def write(near, rows, total):
                ch_snd[index, near, :] = total.astype(BF)

            combine(h, write, to_slot(dz), c, start, 128, extras)
            copy = remote(
                ch_snd.at[index], ch_rcv.at[index], ch_s.at[index], ch_r.at[index], device
            )
            copy.start()
            ch_copies[h, ch, k] = copy

    def finish(h):
        own = pair_ready(h, 0)
        for start, last, side in ((0, (0, 3), (3, 2)), (128, (2, 3), (1, 2))):
            ch_copies[(h,) + side].wait_recv()
            ch_copies[(h,) + last].wait_recv()

            def write(near, rows, total):
                low = total.astype(BF)
                zr, zi = low[:, :HALF], low[:, HALF:]
                lower = pl.ds(pl.multiple_of(rows.start + NB, 32), 32)
                left = slice(h * HALF, (h + 1) * HALF)
                right = slice(NB + h * HALF, NB + (h + 1) * HALF)
                zblk[rows, left] = zr
                zblk[rows, right] = zi
                zblk[lower, left] = -zi
                zblk[lower, right] = zr

            combine(
                h, write, z, c, start, 128,
                [(own, False)] + [
                    (ch_rcv.at[(h * 4 + ch) * 4 + k], True) for ch, k in (side, last)
                ],
            )

    gathered(0, 1)
    multiply(0, 0, 8)
    pair_send(0, 4, 3, -3)
    chain_steps(0, 0)
    pair_send(0, 2, -2)
    gathered(1, 1)
    multiply(1, 0, 2)
    chain_steps(0, 1)
    pair_send(0, 1, -1, 0)
    multiply(1, 2, 4)
    chain_steps(0, 2)
    multiply(1, 4, 6)
    chain_steps(0, 3)
    multiply(1, 6, 8)
    pair_send(1, 4, 3, -3)
    chain_steps(1, 0)
    finish(0)
    pair_send(1, 2, -2)
    chain_steps(1, 1)
    pair_send(1, 1, -1, 0)
    chain_steps(1, 2)
    chain_steps(1, 3)
    finish(1)

    sent1 = recv1.at[pl.ds(0, PLANE - 1)]
    remote(sent1, sent1, s1_s, s1_r, partner).wait_send()
    sent3 = recv2.at[pl.ds(0, 2 * (2 * NZ - 1))]
    remote(sent3, sent3, s3_s, s1_r, partner).wait_send()
    for copy in k_copies + started:
        copy.wait_send()
    for copy in list(pair_copies.values()) + list(ch_copies.values()):
        copy.wait_send()


def reduced(test_points, test_basis, source_points, source_basis, excitation, plan, owner):
    vmem = pl.BlockSpec(memory_space=pltpu.VMEM)
    smem = pl.BlockSpec(memory_space=pltpu.SMEM)
    hbm = pl.BlockSpec(memory_space=pl.ANY)
    dma = pltpu.SemaphoreType.DMA
    scratch = [
        pltpu.VMEM((2, PTS, NB), BF),
        pltpu.VMEM((2, NB, NB), BF),
        pltpu.VMEM((2, 16, 64, NB), BF),
        pltpu.VMEM((PLANE, 64, NB), BF),
        pltpu.VMEM((4 * NZ, 16, 128), BF),
        pltpu.VMEM((4 * NZ, 16, 128), BF),
        pltpu.VMEM((4, 16, 128), BF),
        pltpu.VMEM((2, 2, NY, NX, 64, NB), BF),
        pltpu.VMEM((PLANE, 3, PTS), BF),
        pltpu.VMEM((2, 3, PTS), BF),
        pltpu.VMEM((NZ, 2, 3, PTS), BF),
        pltpu.VMEM((2, 3, PTS), BF),
        pltpu.VMEM((2, 2, PTS, NB), BF),
        pltpu.VMEM((2, 4), jnp.int32),
        pltpu.SMEM((2, 4), jnp.int32),
        pltpu.VMEM((32, PTS), F32),
        pltpu.VMEM((2, 32, PTS), BF),
        pltpu.VMEM((2, 32, PTS), BF),
        pltpu.VMEM((256, PTS), F32),
        pltpu.VMEM((2, 2 * PTS, PTS), BF),
        pltpu.VMEM((2, 2 * PTS, PTS), BF),
        pltpu.VMEM((2, 9, NB, NB), F32),
        pltpu.VMEM((2 * NZ, NB, NB), BF),
        pltpu.VMEM((2 * NZ, NB, NB), BF),
        pltpu.VMEM((32, 128, NB), BF),
        pltpu.VMEM((32, 128, NB), BF),
        pltpu.SMEM((4 * 2 * NZ,), jnp.int32),
        dma, dma, dma, dma, dma, dma, dma, dma, dma, dma((2,)),
        dma((24,)), dma((24,)), dma((3,)), dma((3,)),
        dma((2 * NZ,)), dma((2 * NZ,)), dma((32,)), dma((32,)), dma((4,)),
    ]
    return pl.pallas_call(
        body,
        out_shape=jax.ShapeDtypeStruct((2 * NB, 2 * NB), BF),
        in_specs=[smem, smem, vmem, vmem, hbm, vmem, hbm, hbm],
        out_specs=vmem,
        scratch_shapes=scratch,
        compiler_params=pltpu.CompilerParams(
            collective_id=0, has_side_effects=True, vmem_limit_bytes=60 * 1024 * 1024
        ),
    )(plan, owner, owner, test_points, test_basis, source_points, source_basis, excitation)


def shards(
    test_points,
    test_basis,
    source_points,
    source_basis,
    excitation,
    preconditioner,
    plan,
    solver_owner,
):
    block = reduced(
        test_points[0], test_basis[0], source_points[0], source_basis[0], excitation[0],
        plan, solver_owner[0],
    )
    rows = preconditioner[0].reshape(NB, 2 * NB)
    outcome = jnp.dot(rows, block, preferred_element_type=F32)
    return outcome.reshape(1, NB, 2, NB)


def solution(mesh):
    return jax.shard_map(
        shards,
        mesh=mesh,
        in_specs=(
            P(("group", "member"), None, None),
            P(("group", "member"), None, None, None),
            P(("group", "member"), None, None),
            P(("group", "member"), None, None, None),
            P(("group", "member"), None, None, None),
            P(("group", "member"), None, None, None),
            P(),
            P(("group", "member"), None, None),
        ),
        out_specs=P(("group", "member"), None, None, None),
        check_vma=False,
    )
```

time: 107 us -> 103 us (0.963)
  Pallas kernels: 104 us -> 99.3 us
    pallas_call x1, Pallas kernels: 104 us -> 99.3 us  [reduced(): pl.pallas_call(body, out_shape=jax.ShapeDtypeStruct((2 * NB, 2 * NB), BF)...]
where the time goes in v2:
time: 103 us
  Pallas kernels  99.3 us (96%)
  local copies, waits for them, and re-layouts  1.98 us (2%)
  matrix products  1.39 us (1%)
    pallas_call x1, Pallas kernels, reduced(): pl.pallas_call(body, out_shape=jax.ShapeDtypeStruct((2 * NB, 2 * NB), BF)...  99.3 us

profile of v2, /device:TPU:1, one launch (start us, length us, event | category | flops | bytes accessed | tf_op | source)
XLA Modules:
  0.0 102.7 jit_solution(3358953166451165743)
XLA Ops:
  0.0 1.0 copy.10
  1.0 99.3 %shard_map.82 = bf16[512,512]{1,0:T(8,128)(2,1)} custom-call(s32[2,2]{1,0:T(2,128)} %plan.1, s32[2,4]{1,0:T(2,128)} %bitcast.22, s32[2,4]{1,0:T(2,128)} %bitcast.23, bf16[3,1024]{1,0:T(4,128)(2,1)} %bitcast.20, bf16[2,1024,256]{2,1,0:T(8,128)(2,1)} %bitcast.15, bf16[3,1024]{1,0:T(4,128)(2,1)} %bitcast.21, bf16[2,1024,256]{2,1,0:T(8,128)(2,1)} %bitcast.16, ...), custom_call_target="tpu_custom_call" | custom-call | tf_op jit(solution)/shard_map/pallas_call | solution.py:519
  100.3 1.4 %fusion = f32[512,256]{1,0:T(8,128)S(1)} fusion(bf16[512,512]{1,0:T(8,128)(2,1)} %shard_map.82, bf16[256,512]{1,0:T(8,128)(2,1)S(1)} %bitcast.17), kind=kOutput, calls=%fused_computation | convolution fusion | flops 134217728 | bytes 1310720 | tf_op jit(solution)/shard_map/dot_general | solution.py:546
  101.7 1.0 copy.9

commit v3 on v2

--- a/solution.py
+++ b/solution.py
@@ -66,7 +66,7 @@
     zblk,
     jb, xb, bundle, recv1, sel, recv2, fin, full,
     pt_recv, pt_sel, pt_z, test_all, kall, owner_rem, owner_other,
-    aug_stage, aug_test, aug_src, d2buf, gre, gim, prod,
+    aug_stage, aug_test, aug_src, d2buf, gre, gim, half, prod,
     pair_snd, pair_rcv, ch_snd, ch_rcv, table,
     p1_s, p1_r, s1_s, s1_r, p2_s, p2_r, s2_s, s2_r, s3_s, s3_r,
     s4_s, s4_r, k_s, k_r, pair_s, pair_r, ch_s, ch_r, loc,
@@ -191,28 +191,6 @@
     def recv_bytes(ref, recv):
         remote(ref, ref, s1_s, recv, partner).wait_recv()
 
-    recv_bytes(recv1.at[pl.ds(0, PLANE - 1)], s1_r)
-    keep.wait()
-    for j in range(4):
-        qj = plane_of(plan[j // 2, j % 2])
-        for zp in range(NZ):
-            r0, c0 = (zp % 4) * 16, (zp // 4) * 128
-            sel[zp * 4 + j] = recv1[qj, r0:r0 + 16, c0:c0 + 128]
-
-    @pl.loop(1, NZ)
-    def _(i):
-        tz = lax.rem(z + i, NZ)
-        remote(
-            sel.at[pl.ds(tz * 4, 4)], recv2.at[pl.ds(z * 4, 4)], s2_s, s2_r, (g, tz * 2 + c)
-        ).start()
-
-    recv2[pl.ds(z * 4, 4)] = sel[pl.ds(z * 4, 4)]
-
-    wait_bytes(pt_z.at[pl.ds(0, NZ - 1)], p2_s, p2_r)
-    for s in range(2):
-        augment(pt_z[z_of(plan[c, s]), s], aug_stage, True)
-        aug_src[s] = aug_stage[...].astype(BF)
-
     def green(first, last):
         @pl.loop(first, last)
         def _(unit):
@@ -225,12 +203,12 @@
             )
             base = rest * 256
 
-            @pl.loop(0, 16)
+            @pl.loop(0, 8)
             def _(r):
-                row = pl.ds(pl.multiple_of(r * 16, 16), 16)
-                out = pl.ds(pl.multiple_of(base + r * 16, 16), 16)
-                for col in range(0, PTS, 512):
-                    d2 = jnp.maximum(d2buf[row, col:col + 512], RADIUS_SQ)
+                row = pl.ds(pl.multiple_of(r * 32, 32), 32)
+                out = pl.ds(pl.multiple_of(base + r * 32, 32), 32)
+                for col in range(0, PTS, 256):
+                    d2 = jnp.maximum(d2buf[row, col:col + 256], RADIUS_SQ)
                     inv = lax.rsqrt(d2)
                     dist = d2 * inv
                     f = dist - jnp.round(dist)
@@ -239,10 +217,31 @@
                     cs = poly(COS, u)
                     t = (inv * (0.5 / math.pi)) * sn
                     re = inv * (0.25 / math.pi) - t * sn
-                    gre[s, out, col:col + 512] = re.astype(BF)
-                    gim[s, out, col:col + 512] = (t * cs).astype(BF)
-
-    green(0, 2)
+                    gre[s, out, col:col + 256] = re.astype(BF)
+                    gim[s, out, col:col + 256] = (t * cs).astype(BF)
+
+    recv_bytes(recv1.at[pl.ds(0, PLANE - 1)], s1_r)
+    keep.wait()
+    for j in range(4):
+        qj = plane_of(plan[j // 2, j % 2])
+        for zp in range(NZ):
+            r0, c0 = (zp % 4) * 16, (zp // 4) * 128
+            sel[zp * 4 + j] = recv1[qj, r0:r0 + 16, c0:c0 + 128]
+
+    @pl.loop(1, NZ)
+    def _(i):
+        tz = lax.rem(z + i, NZ)
+        remote(
+            sel.at[pl.ds(tz * 4, 4)], recv2.at[pl.ds(z * 4, 4)], s2_s, s2_r, (g, tz * 2 + c)
+        ).start()
+
+    recv2[pl.ds(z * 4, 4)] = sel[pl.ds(z * 4, 4)]
+
+    wait_bytes(pt_z.at[pl.ds(0, NZ - 1)], p2_s, p2_r)
+    for s in range(2):
+        augment(pt_z[z_of(plan[c, s]), s], aug_stage, True)
+        aug_src[s] = aug_stage[...].astype(BF)
+
 
     wait_bytes(recv2.at[pl.ds(0, 4 * (NZ - 1))], s2_s, s2_r)
     for j in range(4):
@@ -288,18 +287,13 @@
         for copy in arriving[h, stage]:
             copy.wait_recv()
 
-    green(2, 6)
+    green(0, 16)
     recv_bytes(recv2.at[pl.ds(0, 2 * NZ)], s3_r.at[0])
     gather(0, 0)
-    green(6, 8)
     recv_bytes(recv2.at[pl.ds(0, 2 * NZ)], s3_r.at[1])
     gather(1, 0)
     gathered(0, 0)
     gather(0, 1)
-    green(8, 11)
-    gathered(1, 0)
-    gather(1, 1)
-    green(11, 16)
 
     k_copies[1].wait_recv()
     scal = pltpu.make_async_copy(owner_rem, owner_other, loc.at[3])
@@ -330,27 +324,30 @@
 
     k_copies[2].wait_recv()
     k_own.wait()
-
-    def multiply(h, first, last):
-        @pl.loop(first, last)
-        def _(unit):
-            s, dom = lax.div(unit, 4), lax.rem(unit, 4)
-            rows = pl.ds(pl.multiple_of(dom * 512, 512), 512)
-            who = lax.div(dom, 2)
-            krow = pl.ds(pl.multiple_of(lax.rem(dom, 2) * 512, 512), 512)
-            basis = full[s, h].reshape(PTS, NB)
-            one = dot(gre[s, rows, :], basis)
-            two = dot(gim[s, rows, :], basis)
-            half_re = (one[:, :HALF] + two[:, HALF:]).astype(BF)
-            half_im = (one[:, HALF:] - two[:, :HALF]).astype(BF)
-            right = jnp.concatenate([half_re, half_im], axis=1)
-            turned = jnp.concatenate([half_im, -half_re], axis=1)
-            over = (((0,), (0,)), ((), ()))
-            prod[h, unit] = lax.dot_general(
-                kall[who, 0, krow, :], right, over, preferred_element_type=F32
-            ) + lax.dot_general(
-                kall[who, 1, krow, :], turned, over, preferred_element_type=F32
-            )
+    gathered(1, 0)
+
+    def field(h, unit):
+        s, dom = lax.div(unit, 4), lax.rem(unit, 4)
+        rows = pl.ds(pl.multiple_of(dom * 512, 512), 512)
+        basis = full[s, h].reshape(PTS, NB)
+        return dot(gre[s, rows, :], basis), dot(gim[s, rows, :], basis)
+
+    def keep_field(slot, one, two):
+        half[slot, :, :HALF] = (one[:, :HALF] + two[:, HALF:]).astype(BF)
+        half[slot, :, HALF:] = (one[:, HALF:] - two[:, :HALF]).astype(BF)
+
+    def project(h, unit, slot):
+        dom = lax.rem(unit, 4)
+        who = lax.div(dom, 2)
+        krow = pl.ds(pl.multiple_of(lax.rem(dom, 2) * 512, 512), 512)
+        right = half[slot]
+        turned = jnp.concatenate([right[:, HALF:], -right[:, :HALF]], axis=1)
+        over = (((0,), (0,)), ((), ()))
+        prod[h, unit] = lax.dot_general(
+            kall[who, 0, krow, :], right, over, preferred_element_type=F32
+        ) + lax.dot_general(
+            kall[who, 1, krow, :], turned, over, preferred_element_type=F32
+        )
 
     def combine(h, write, zz, cc, start, count, extras):
         base = (zz * 2 + cc) * 4
@@ -366,116 +363,141 @@
                 total = total + ref[near if shifted else rows, :].astype(F32)
             write(near, rows, total)
 
-    def to_slot(dz):
-        return lax.rem(z + dz + NZ, NZ)
-
-    pair_copies = {}
-    waited = set()
-
-    def pair_send(h, *distances):
-        for dz in distances:
-            index = h * NZ + dz % NZ
+    def pair_copy(h, dz):
+        index = h * NZ + dz
+        return remote(
+            pair_snd.at[index], pair_rcv.at[index],
+            pair_s.at[index], pair_r.at[index], partner,
+        )
+
+    def pair_all(h):
+        @pl.loop(0, NZ)
+        def _(i):
+            dz = 4 + lax.div(i + 1, 2) * (1 - 2 * lax.rem(i, 2))
 
             def write(near, rows, total):
-                pair_snd[index, rows, :] = total.astype(BF)
-
-            combine(h, write, to_slot(dz), other, 0, NB, ())
-            copy = remote(
-                pair_snd.at[index], pair_rcv.at[index],
-                pair_s.at[index], pair_r.at[index], partner,
+                pair_snd[h * NZ + dz, rows, :] = total.astype(BF)
+
+            combine(h, write, lax.rem(z + dz, NZ), other, 0, NB, ())
+            pair_copy(h, dz).start()
+
+    neighbours = (
+        (g, lax.rem(z + 1, NZ) * 2 + c),
+        (g, lax.rem(z + NZ - 1, NZ) * 2 + c),
+    )
+
+    def chain_base(h, side, pair):
+        return ((h * 2 + side) * 2 + pair) * 5
+
+    def chain_copy(index, side):
+        return remote(
+            ch_snd.at[index], ch_rcv.at[index + 1],
+            ch_s.at[index], ch_r.at[index + 1], neighbours[side],
+        )
+
+    def chain_step(h, step):
+        k, pair = lax.div(step, 2), lax.rem(step, 2)
+        for side in range(2):
+            far = 4 - pair - k
+            dz = far if side == 0 else NZ - far
+            start = 128 * pair if side == 0 else 128 * (1 - pair)
+            index = chain_base(h, side, pair) + k
+            fresh = step == 0 if side == 0 else step < 0
+
+            @pl.when(jnp.logical_or(pair == 1, fresh))
+            def _(dz=dz):
+                pair_copy(h, dz).wait_recv()
+
+            @pl.when(k > 0)
+            def _(index=index, side=side):
+                chain_copy(index - 1, side).wait_recv()
+
+            def write(near, rows, total, index=index):
+                ch_snd[index, near, :] = total.astype(BF)
+
+            combine(
+                h, write, lax.rem(z + dz, NZ), c, start, 128,
+                [(pair_rcv.at[h * NZ + dz], False), (ch_rcv.at[index], True)],
             )
-            copy.start()
-            pair_copies[index] = copy
-
-    def pair_ready(h, dz):
-        index = h * NZ + dz % NZ
-        if index not in waited:
-            waited.add(index)
-            pair_copies[index].wait_recv()
-        return pair_rcv.at[index]
-
-    ahead = (g, lax.rem(z + 1, NZ) * 2 + c)
-    behind = (g, lax.rem(z + NZ - 1, NZ) * 2 + c)
-    chains = ((4, 0, ahead), (3, 128, ahead), (-4, 128, behind), (-3, 0, behind))
-    ch_copies = {}
-
-    def chain_steps(h, k):
-        for ch in (0, 2, 1, 3):
-            far, start, device = chains[ch]
-            if k >= abs(far):
-                continue
-            dz = far - k if far > 0 else far + k
-            extras = [(pair_ready(h, dz), False)]
-            index = (h * 4 + ch) * 4 + k
-            if k:
-                ch_copies[h, ch, k - 1].wait_recv()
-                extras.append((ch_rcv.at[index - 1], True))
-
-            def write(near, rows, total):
-                ch_snd[index, near, :] = total.astype(BF)
-
-            combine(h, write, to_slot(dz), c, start, 128, extras)
-            copy = remote(
-                ch_snd.at[index], ch_rcv.at[index], ch_s.at[index], ch_r.at[index], device
-            )
-            copy.start()
-            ch_copies[h, ch, k] = copy
+            chain_copy(index, side).start()
 
     def finish(h):
-        own = pair_ready(h, 0)
-        for start, last, side in ((0, (0, 3), (3, 2)), (128, (2, 3), (1, 2))):
-            ch_copies[(h,) + side].wait_recv()
-            ch_copies[(h,) + last].wait_recv()
+        pair_copy(h, 0).wait_recv()
+        for part in range(2):
+            last = chain_base(h, part, 0) + 4
+            cross = chain_base(h, 1 - part, 1) + 3
+            chain_copy(last - 1, part).wait_recv()
+            chain_copy(cross - 1, 1 - part).wait_recv()
 
             def write(near, rows, total):
                 low = total.astype(BF)
                 zr, zi = low[:, :HALF], low[:, HALF:]
                 lower = pl.ds(pl.multiple_of(rows.start + NB, 32), 32)
-                left = slice(h * HALF, (h + 1) * HALF)
-                right = slice(NB + h * HALF, NB + (h + 1) * HALF)
+                left = pl.ds(pl.multiple_of(h * HALF, HALF), HALF)
+                right = pl.ds(pl.multiple_of(NB + h * HALF, HALF), HALF)
                 zblk[rows, left] = zr
                 zblk[rows, right] = zi
                 zblk[lower, left] = -zi
                 zblk[lower, right] = zr
 
             combine(
-                h, write, z, c, start, 128,
-                [(own, False)] + [
-                    (ch_rcv.at[(h * 4 + ch) * 4 + k], True) for ch, k in (side, last)
-                ],
+                h, write, z, c, 128 * part, 128,
+                [(pair_rcv.at[h * NZ], False), (ch_rcv.at[last], True), (ch_rcv.at[cross], True)],
             )
 
+    @pl.loop(0, 8)
+    def _(i):
+        ch_rcv[i * 5] = jnp.zeros((128, NB), BF)
+
     gathered(0, 1)
-    multiply(0, 0, 8)
-    pair_send(0, 4, 3, -3)
-    chain_steps(0, 0)
-    pair_send(0, 2, -2)
-    gathered(1, 1)
-    multiply(1, 0, 2)
-    chain_steps(0, 1)
-    pair_send(0, 1, -1, 0)
-    multiply(1, 2, 4)
-    chain_steps(0, 2)
-    multiply(1, 4, 6)
-    chain_steps(0, 3)
-    multiply(1, 6, 8)
-    pair_send(1, 4, 3, -3)
-    chain_steps(1, 0)
-    finish(0)
-    pair_send(1, 2, -2)
-    chain_steps(1, 1)
-    pair_send(1, 1, -1, 0)
-    chain_steps(1, 2)
-    chain_steps(1, 3)
-    finish(1)
+    gather(1, 1)
+
+    @pl.loop(0, 17)
+    def _(step):
+        @pl.when(step == 8)
+        def _():
+            gathered(1, 1)
+
+        now = jnp.minimum(step, 15)
+        old = jnp.maximum(step - 1, 0)
+        one, two = field(lax.div(now, 8), lax.rem(now, 8))
+        project(lax.div(old, 8), lax.rem(old, 8), lax.rem(step + 1, 2))
+        keep_field(lax.rem(step, 2), one, two)
+
+        @pl.when(step == 8)
+        def _():
+            pair_all(0)
+
+        @pl.when(jnp.logical_and(step > 8, step < 16))
+        def _():
+            chain_step(0, step - 9)
+
+    pair_all(1)
+
+    @pl.loop(0, 7)
+    def _(step):
+        chain_step(1, step)
+
+    @pl.loop(0, 2)
+    def _(h):
+        finish(h)
+
+    @pl.loop(0, 2 * NZ)
+    def _(i):
+        pair_copy(0, i).wait_send()
+
+    @pl.loop(0, 14)
+    def _(i):
+        h, step = lax.div(i, 7), lax.rem(i, 7)
+        for side in range(2):
+            index = chain_base(h, side, lax.rem(step, 2)) + lax.div(step, 2)
+            chain_copy(index, side).wait_send()
 
     sent1 = recv1.at[pl.ds(0, PLANE - 1)]
     remote(sent1, sent1, s1_s, s1_r, partner).wait_send()
     sent3 = recv2.at[pl.ds(0, 2 * (2 * NZ - 1))]
     remote(sent3, sent3, s3_s, s1_r, partner).wait_send()
     for copy in k_copies + started:
-        copy.wait_send()
-    for copy in list(pair_copies.values()) + list(ch_copies.values()):
         copy.wait_send()
 
 
@@ -506,15 +528,16 @@
         pltpu.VMEM((256, PTS), F32),
         pltpu.VMEM((2, 2 * PTS, PTS), BF),
         pltpu.VMEM((2, 2 * PTS, PTS), BF),
+        pltpu.VMEM((2, 512, NB), BF),
         pltpu.VMEM((2, 9, NB, NB), F32),
         pltpu.VMEM((2 * NZ, NB, NB), BF),
         pltpu.VMEM((2 * NZ, NB, NB), BF),
-        pltpu.VMEM((32, 128, NB), BF),
-        pltpu.VMEM((32, 128, NB), BF),
+        pltpu.VMEM((40, 128, NB), BF),
+        pltpu.VMEM((40, 128, NB), BF),
         pltpu.SMEM((4 * 2 * NZ,), jnp.int32),
         dma, dma, dma, dma, dma, dma, dma, dma, dma, dma((2,)),
         dma((24,)), dma((24,)), dma((3,)), dma((3,)),
-        dma((2 * NZ,)), dma((2 * NZ,)), dma((32,)), dma((32,)), dma((4,)),
+        dma((2 * NZ,)), dma((2 * NZ,)), dma((40,)), dma((40,)), dma((4,)),
     ]
     return pl.pallas_call(
         body,

time: 103 us -> 114 us (1.11)
  Pallas kernels: 99.3 us -> 110 us
    pallas_call x1, Pallas kernels: 99.3 us -> 110 us  [reduced(): pl.pallas_call(body, out_shape=jax.ShapeDtypeStruct((2 * NB, 2 * NB), BF)...]
where the time goes in v3:
time: 114 us; the launch traced here: 113 us
  Pallas kernels  110 us (96%)
  local copies, waits for them, and re-layouts  1.98 us (2%)
  matrix products  1.39 us (1%)
    pallas_call x1, Pallas kernels, reduced(): pl.pallas_call(body, out_shape=jax.ShapeDtypeStruct((2 * NB, 2 * NB), BF)...  110 us

profile of v3, /device:TPU:1, one launch (start us, length us, event | category | flops | bytes accessed | tf_op | source)
XLA Modules:
  0.0 113.3 jit_solution(17978953522797714272)
XLA Ops:
  0.0 1.0 copy.10
  1.0 109.9 %shard_map.82 = bf16[512,512]{1,0:T(8,128)(2,1)} custom-call(s32[2,2]{1,0:T(2,128)} %plan.1, s32[2,4]{1,0:T(2,128)} %bitcast.22, s32[2,4]{1,0:T(2,128)} %bitcast.23, bf16[3,1024]{1,0:T(4,128)(2,1)} %bitcast.20, bf16[2,1024,256]{2,1,0:T(8,128)(2,1)} %bitcast.15, bf16[3,1024]{1,0:T(4,128)(2,1)} %bitcast.21, bf16[2,1024,256]{2,1,0:T(8,128)(2,1)} %bitcast.16, ...), custom_call_target="tpu_custom_call" | custom-call | tf_op jit(solution)/shard_map/pallas_call | solution.py:542
  110.9 1.4 %fusion = f32[512,256]{1,0:T(8,128)S(1)} fusion(bf16[512,512]{1,0:T(8,128)(2,1)} %shard_map.82, bf16[256,512]{1,0:T(8,128)(2,1)S(1)} %bitcast.17), kind=kOutput, calls=%fused_computation | convolution fusion | flops 134217728 | bytes 1310720 | tf_op jit(solution)/shard_map/dot_general | solution.py:569
  112.3 1.0 copy.9
